TPU v7x, 32 devices: a whole 2x2x4 slice. The times are simulated.
32 devices in a mesh: tm: 8 (over z, x), space: 4 (over y, core).
Axes of the slice: x: 2, y: 2, z: 4, core: 2. Of those that a mesh axis runs over, the one named last changes fastest.
Arguments:
- snapshots: float32 [4224, 4096], P('tm', 'space')
- starts: int32 [32], replicated, may hold values from 0 to 3968, as said below
- freq_lines: int32 [128], replicated, may hold values from 0 to 128, as said below
Outputs:
- power_density: float32 [128, 4096], P(None, ('space', 'tm'))
- gram_matrices: float32 [2, 128, 32, 32], P(None, 'tm')
Inputs may be any that keep to these rules, and one draw needn't show every extreme that they name: starts never fall, and block b starts at most 64 snapshots away from b * 128; the first block starts at 0 and the last at 3968. `freq_lines`: distinct line numbers in any order; 0 and 128 are among them.
All inputs are finite; a program needn't handle non-finite values.
Results may differ from a plain program's by a relative error of at most 0.0001.
Values sent between devices are 32-bit elements; how exact they have to be, the bound alone decides.
No kernel may reach another device: no remote copies, remote signals or barrier semaphores. Data moves between devices by JAX's collectives and lax.ppermute only.
A program may use at most 64 MiB of HBM per device.

v0:
```python
import math
import jax
import jax.numpy as jnp
from jax import lax
from jax.sharding import PartitionSpec as P

NFFT = 256
NF = 128
NB = 32


def spectral_table(freq_lines):
    moments = jnp.arange(NFFT, dtype=jnp.int32)
    cycle = freq_lines[:, None] * moments[None, :] % NFFT
    angles = 2.0 * math.pi / NFFT * cycle.astype(jnp.float32)
    window = 0.5 - 0.5 * jnp.cos(2.0 * math.pi / NFFT * moments.astype(jnp.float32))
    window = window / jnp.sqrt(jnp.sum(window * window))
    return jnp.concatenate(
        [window[None, :] * jnp.cos(angles), -window[None, :] * jnp.sin(angles)], axis=0
    )


def block_spectra(series, starts, table):
    offsets = starts[:, None] + jnp.arange(NFFT, dtype=jnp.int32)[None, :]
    blocks = series[offsets]
    return jnp.einsum("kt,btp->kbp", table, blocks, precision=lax.Precision.HIGHEST)


def local_terms(spectra, factor):
    highest = lax.Precision.HIGHEST
    real_part = spectra[:NF]
    imag_part = spectra[NF:]
    power = jnp.sum(real_part * real_part + imag_part * imag_part, axis=1) / NB
    gram_real = jnp.einsum("fbp,fcp->fbc", real_part, real_part, precision=highest) + jnp.einsum(
        "fbp,fcp->fbc", imag_part, imag_part, precision=highest
    )
    gram_imag = jnp.einsum("fbp,fcp->fbc", real_part, imag_part, precision=highest) - jnp.einsum(
        "fbp,fcp->fbc", imag_part, real_part, precision=highest
    )
    return (power, jnp.stack([gram_real, gram_imag]) * factor)


def body(snapshots, starts, freq_lines):
    groups = lax.axis_size("tm")
    columns = snapshots.shape[1] // groups
    table = spectral_table(freq_lines)
    arranged = snapshots.reshape(snapshots.shape[0], groups, columns)
    spectra = block_spectra(
        lax.all_to_all(arranged, "tm", split_axis=1, concat_axis=0, tiled=True)[:, 0, :],
        starts,
        table,
    )
    total_points = columns * groups * lax.axis_size("space")
    power_density, own_gram = local_terms(spectra, 1.0 / (NB * total_points))
    per_device = NF // groups
    summed = lax.psum(own_gram, ("tm", "space"))
    gram_matrices = lax.dynamic_slice_in_dim(
        summed, lax.axis_index("tm") * per_device, per_device, 1
    )
    return (power_density, gram_matrices)


def solution(mesh):
    placed = (P("tm", "space"), P(), P())
    return jax.shard_map(
        body,
        mesh=mesh,
        in_specs=placed,
        out_specs=(P(None, ("space", "tm")), P(None, "tm", None, None)),
        check_vma=False,
    )
```

profile of v0, /device:TPU:0, one launch (start us, length us, event | category | flops | bytes accessed | tf_op | source)
XLA Modules:
  0.0 276.6 jit_solution(2760193698736418181)
XLA Ops:
  7.2 0.0 copy-start
  7.2 1.6 copy-done
  8.8 1.5 copy_bitcast_fusion
  10.3 0.0 copy-start.2
  10.3 0.0 copy-start.3
  10.3 7.4 %all-to-all-start = ((f32[528,8,128]{2,0,1:T(8,128)}), f32[528,8,128]{2,0,1:T(8,128)}, u32[]{:S(2)}, u32[]{:S(2)}) async-start(f32[528,8,128]{2,0,1:T(8,128)} %copy_bitcast_fusion), calls=%async_computation | async-start | bytes 4325376 | tf_op jit(solution)/shard_map/all_to_all | solution.py:49
  17.7 0.0 all-reduce.2.cloned.1.call-start
  17.7 0.6 multiply_reduce_fusion
  19.1 0.0 copy-done.2
  19.1 0.1 fusion.25
  19.2 0.0 copy-done.3
  19.2 0.6 cosine_multiply_fusion
  19.9 47.6 %all-to-all-done = f32[528,8,128]{2,0,1:T(8,128)} async-done(((f32[528,8,128]{2,0,1:T(8,128)}), f32[528,8,128]{2,0,1:T(8,128)}, u32[]{:S(2)}, u32[]{:S(2)}) %all-to-all-start) | async-done | bytes 2162720 | tf_op jit(solution)/shard_map/all_to_all | solution.py:49
  67.4 29.4 %gather_fusion = f32[8192,128]{1,0:T(8,128)} fusion(f32[4224,128]{1,0:T(8,128)} %bitcast.3, s32[8192]{0:T(1024)S(1)} %broadcast_clamp_fusion), kind=kCustom, calls=%fused_computation | custom fusion | bytes 8421376 | tf_op jit(solution)/shard_map/gather | solution.py:25
  96.8 5.6 %fusion.16 = f32[256,32,128]{2,0,1:T(8,128)S(1)} fusion(f32[32,256,128]{2,1,0:T(8,128)} %bitcast.23, f32[128,256]{1,0:T(8,128)S(1)} %get-tuple-element.8, f32[128,256]{1,0:T(8,128)S(1)} %get-tuple-element.7), kind=kOutput, calls=%fused_computation.17 | convolution fusion | flops 3221291008 | bytes 8650752 | tf_op jit(solution)/shard_map/kt,btp->kbp/dot_general | solution.py:26
  102.4 0.7 fusion.29
  103.1 0.0 copy-start.1
  103.1 5.7 %fusion.4 = f32[128,32,32]{2,1,0:T(8,128)} fusion(f32[128,32,128]{2,0,1:T(8,128)S(1)} %get-tuple-element.6), kind=kOutput, calls=%fused_computation.9 | convolution fusion | flops 201326592 | bytes 2621440 | tf_op jit(solution)/shard_map/fbp,fcp->fbc/dot_general | solution.py:34
  108.8 5.7 %fusion = f32[128,32,32]{2,1,0:T(8,128)S(1)} fusion(f32[128,32,128]{2,0,1:T(8,128)S(1)} %get-tuple-element.6, f32[128,32,128]{2,0,1:T(8,128)S(1)} %get-tuple-element.4), kind=kOutput, calls=%fused_computation.5 | convolution fusion | flops 201326592 | bytes 4718592 | tf_op jit(solution)/shard_map/fbp,fcp->fbc/dot_general | solution.py:37
  114.5 0.0 copy-done.1
  114.5 7.2 %subtract_bitcast_fusion = f32[1,128,32,32]{3,2,1,0:T(8,128)} fusion(f32[128,32,32]{2,1,0:T(8,128)S(1)} %fusion, f32[128,32,128]{2,0,1:T(8,128)S(1)} %get-tuple-element.6, f32[128,32,128]{2,0,1:T(8,128)S(1)} %get-tuple-element.4), kind=kOutput, calls=%fused_computation.2 | convolution fusion | flops 201457664 | bytes 5242880 | tf_op jit(solution)/shard_map/fbp,fcp->fbc/dot_general | solution.py:37
  121.7 2.7 copy.33
  124.3 9.7 %add_bitcast_fusion = f32[1,128,32,32]{3,2,1,0:T(8,128)} fusion(f32[128,32,32]{2,1,0:T(8,128)} %fusion.4, f32[128,32,128]{2,0,1:T(8,128)} %copy-done.1), kind=kOutput, calls=%fused_computation.3 | convolution fusion | flops 201457664 | bytes 3145728 | tf_op jit(solution)/shard_map/fbp,fcp->fbc/dot_general | solution.py:34
  134.1 2.7 copy.32
  136.7 1.1 maximum_multiply_fusion
  137.8 0.0 all-reduce.2.cloned.1.call-update
  137.9 0.6 broadcast_multiply_fusion
  138.5 128.4 %all-reduce.2.cloned.1.call-done = f32[2,128,32,32]{1,3,2,0:T(8,128)} async-done(((f32[2,128,32,32]{1,3,2,0:T(8,128)}), f32[2,128,32,32]{1,3,2,0:T(8,128)}) %all-reduce.2.cloned.1.call-update) | async-done | bytes 1048592 | tf_op jit(solution)/shard_map/psum | solution.py:56
  266.9 1.6 constant_dynamic-slice_fusion
  268.5 1.2 copy.34
  (3 shorter events, 0.1 us)
Async XLA Ops:
  7.2 1.6 copy-start
  10.3 8.8 %copy-start.2 = (s32[32]{0:T(128)S(1)}, s32[32]{0:T(128)}, u32[]{:S(2)}) copy-start(s32[32]{0:T(128)} %param.4) | copy-start | bytes 388
  10.3 9.0 %copy-start.3 = (s32[128]{0:T(128)S(1)}, s32[128]{0:T(128)}, u32[]{:S(2)}) copy-start(s32[128]{0:T(128)} %param.5) | copy-start | bytes 1540
  10.3 57.1 %all-to-all-start = ((f32[528,8,128]{2,0,1:T(8,128)}), f32[528,8,128]{2,0,1:T(8,128)}, u32[]{:S(2)}, u32[]{:S(2)}) async-start(f32[528,8,128]{2,0,1:T(8,128)} %copy_bitcast_fusion), calls=%async_computation | async-start | bytes 4325376 | tf_op jit(solution)/shard_map/all_to_all | solution.py:49
  17.7 249.3 %all-reduce.2.cloned.1.call-start = ((), (), s32[]{:S(2)}) async-start(), calls=%async_computation.1 | async-start | bytes 2097152 | tf_op jit(solution)/shard_map/psum | solution.py:56
  103.1 11.4 %copy-start.1 = (f32[128,32,128]{2,0,1:T(8,128)}, f32[128,32,128]{2,0,1:T(8,128)S(1)}, u32[]{:S(2)}) copy-start(f32[128,32,128]{2,0,1:T(8,128)S(1)} %get-tuple-element.4) | copy-start | bytes 6291460
Sparse Core Ops, SparseCore 0:
  138.0 128.9 all-reduce.1
where the time goes:
time: 277 us
  waiting for transfers between devices  176 us (64%)
  local copies, waits for them, and re-layouts  40.6 us (15%)
  matrix products  33.9 us (12%)
  between operations  14.8 us (5%)
  starting transfers between devices  7.42 us (3%)
  other arithmetic  3.87 us (1%)
    psum x1, waiting for transfers between devices, body(): summed = lax.psum(own_gram, ('tm', 'space'))  128 us
    all_to_all x1, waiting for transfers between devices, body(): lax.all_to_all(arranged, 'tm', split_axis=1, concat_axis=0, tiled=True)  47.6 us
    gather x1, local copies, waits for them, and re-layouts, block_spectra(): blocks = series[offsets]  29.4 us
    dot_general x1, matrix products, local_terms(): jnp.einsum('fbp,fcp->fbc', real_part, real_part, precision=highest)  9.72 us
    all_to_all x1, starting transfers between devices, body(): lax.all_to_all(arranged, 'tm', split_axis=1, concat_axis=0, tiled=True)  7.38 us
    dot_general x1, matrix products, local_terms(): jnp.einsum('fbp,fcp->fbc', real_part, imag_part, precision=highest)  7.21 us
    dot_general x1, matrix products, local_terms(): jnp.einsum('fbp,fcp->fbc', imag_part, imag_part, precision=highest)  5.68 us
    dot_general x1, matrix products, local_terms(): jnp.einsum('fbp,fcp->fbc', imag_part, real_part, precision=highest)  5.67 us
  transfers between devices with their start and end apart: 2, of which 2 were waited for; matrix products, arithmetic and copies ran while one was open for 1% of the time, Pallas kernels for 0%

commit v1 on v0

--- a/solution.py
+++ b/solution.py
@@ -53,7 +53,7 @@
     total_points = columns * groups * lax.axis_size("space")
     power_density, own_gram = local_terms(spectra, 1.0 / (NB * total_points))
     per_device = NF // groups
-    summed = lax.psum(own_gram, ("tm", "space"))
+    summed = jnp.sum(lax.all_gather(own_gram, ("tm", "space")), axis=0)
     gram_matrices = lax.dynamic_slice_in_dim(
         summed, lax.axis_index("tm") * per_device, per_device, 1
     )

time: 277 us -> 355 us (1.28)
  waiting for transfers between devices: 176 us -> 241 us
  other arithmetic: 3.87 us -> 16.1 us
    all_gather x0 -> x1, waiting for transfers between devices: none -> 193 us  [body(): summed = jnp.sum(lax.all_gather(own_gram, ('tm', 'space')), axis=0)]
    psum x1 -> x0, waiting for transfers between devices: 128 us -> none  [body(): summed = lax.psum(own_gram, ('tm', 'space'))]
    reduce_sum x0 -> x1, other arithmetic: none -> 12.3 us  [body(): summed = jnp.sum(lax.all_gather(own_gram, ('tm', 'space')), axis=0)]
where the time goes in v1:
time: 355 us
  waiting for transfers between devices  241 us (68%)
  local copies, waits for them, and re-layouts  41.5 us (12%)
  matrix products  33.9 us (10%)
  other arithmetic  16.1 us (5%)
  between operations  14.8 us (4%)
  starting transfers between devices  7.42 us (2%)
    all_gather x1, waiting for transfers between devices, body(): summed = jnp.sum(lax.all_gather(own_gram, ('tm', 'space')), axis=0)  193 us
    all_to_all x1, waiting for transfers between devices, body(): lax.all_to_all(arranged, 'tm', split_axis=1, concat_axis=0, tiled=True)  47.6 us
    gather x1, local copies, waits for them, and re-layouts, block_spectra(): blocks = series[offsets]  29.4 us
    reduce_sum x1, other arithmetic, body(): summed = jnp.sum(lax.all_gather(own_gram, ('tm', 'space')), axis=0)  12.3 us
    dot_general x1, matrix products, local_terms(): jnp.einsum('fbp,fcp->fbc', real_part, real_part, precision=highest)  9.72 us
    all_to_all x1, starting transfers between devices, body(): lax.all_to_all(arranged, 'tm', split_axis=1, concat_axis=0, tiled=True)  7.38 us
    dot_general x1, matrix products, local_terms(): jnp.einsum('fbp,fcp->fbc', real_part, imag_part, precision=highest)  7.21 us
  transfers between devices with their start and end apart: 2, of which 2 were waited for; matrix products, arithmetic and copies ran while one was open for 1% of the time, Pallas kernels for 0%

profile of v1, /device:TPU:0, one launch (start us, length us, event | category | flops | bytes accessed | tf_op | source)
XLA Modules:
  0.0 354.7 jit_solution(14057747708172758820)
XLA Ops:
  7.2 0.0 copy-start
  7.2 1.6 copy-done
  8.8 1.5 copy_bitcast_fusion
  10.3 0.0 copy-start.2
  10.3 0.0 copy-start.3
  10.3 7.4 %all-to-all-start = ((f32[528,8,128]{2,0,1:T(8,128)}), f32[528,8,128]{2,0,1:T(8,128)}, u32[]{:S(2)}, u32[]{:S(2)}) async-start(f32[528,8,128]{2,0,1:T(8,128)} %copy_bitcast_fusion), calls=%async_computation | async-start | bytes 4325376 | tf_op jit(solution)/shard_map/all_to_all | solution.py:49
  17.7 0.0 all-gather.2.cloned.1.call-start
  17.7 0.0 copy-done.2
  17.7 0.1 fusion.25
  17.8 0.6 multiply_reduce_fusion
  19.2 0.0 copy-done.3
  19.2 0.6 cosine_multiply_fusion
  19.9 47.6 %all-to-all-done = f32[528,8,128]{2,0,1:T(8,128)} async-done(((f32[528,8,128]{2,0,1:T(8,128)}), f32[528,8,128]{2,0,1:T(8,128)}, u32[]{:S(2)}, u32[]{:S(2)}) %all-to-all-start) | async-done | bytes 2162720 | tf_op jit(solution)/shard_map/all_to_all | solution.py:49
  67.4 29.4 %gather_fusion = f32[8192,128]{1,0:T(8,128)} fusion(f32[4224,128]{1,0:T(8,128)} %bitcast.3, s32[8192]{0:T(1024)S(1)} %broadcast_clamp_fusion), kind=kCustom, calls=%fused_computation | custom fusion | bytes 8421376 | tf_op jit(solution)/shard_map/gather | solution.py:25
  96.8 5.6 %fusion.16 = f32[256,32,128]{2,0,1:T(8,128)S(1)} fusion(f32[32,256,128]{2,1,0:T(8,128)} %bitcast.23, f32[128,256]{1,0:T(8,128)S(1)} %get-tuple-element.8, f32[128,256]{1,0:T(8,128)S(1)} %get-tuple-element.7), kind=kOutput, calls=%fused_computation.17 | convolution fusion | flops 3221291008 | bytes 8650752 | tf_op jit(solution)/shard_map/kt,btp->kbp/dot_general | solution.py:26
  102.4 0.7 fusion.29
  103.1 0.0 copy-start.1
  103.1 5.7 %fusion.4 = f32[128,32,32]{2,1,0:T(8,128)} fusion(f32[128,32,128]{2,0,1:T(8,128)S(1)} %get-tuple-element.6), kind=kOutput, calls=%fused_computation.9 | convolution fusion | flops 201326592 | bytes 2621440 | tf_op jit(solution)/shard_map/fbp,fcp->fbc/dot_general | solution.py:34
  108.8 5.7 %fusion = f32[128,32,32]{2,1,0:T(8,128)S(1)} fusion(f32[128,32,128]{2,0,1:T(8,128)S(1)} %get-tuple-element.6, f32[128,32,128]{2,0,1:T(8,128)S(1)} %get-tuple-element.4), kind=kOutput, calls=%fused_computation.5 | convolution fusion | flops 201326592 | bytes 4718592 | tf_op jit(solution)/shard_map/fbp,fcp->fbc/dot_general | solution.py:37
  114.5 0.0 copy-done.1
  114.5 7.2 %subtract_bitcast_fusion = f32[1,1,128,32,32]{4,3,2,1,0:T(8,128)} fusion(f32[128,32,32]{2,1,0:T(8,128)S(1)} %fusion, f32[128,32,128]{2,0,1:T(8,128)S(1)} %get-tuple-element.6, f32[128,32,128]{2,0,1:T(8,128)S(1)} %get-tuple-element.4), kind=kOutput, calls=%fused_computation.2 | convolution fusion | flops 201457664 | bytes 5242880 | tf_op jit(solution)/shard_map/fbp,fcp->fbc/dot_general | solution.py:37
  121.7 2.7 copy.44
  124.3 9.7 %add_bitcast_fusion = f32[1,1,128,32,32]{4,3,2,1,0:T(8,128)} fusion(f32[128,32,32]{2,1,0:T(8,128)} %fusion.4, f32[128,32,128]{2,0,1:T(8,128)} %copy-done.1), kind=kOutput, calls=%fused_computation.3 | convolution fusion | flops 201457664 | bytes 3145728 | tf_op jit(solution)/shard_map/fbp,fcp->fbc/dot_general | solution.py:34
  134.1 2.7 copy.43
  136.7 1.1 maximum_multiply_fusion
  137.8 0.0 all-gather.2.cloned.1.call-update
  137.8 0.6 broadcast_multiply_fusion
  138.5 193.4 %all-gather.2.cloned.1.call-done = f32[32,2,128,32,32]{2,4,3,1,0:T(8,128)} async-done(((f32[1,2,128,32,32]{2,4,3,1,0:T(8,128)}), f32[32,2,128,32,32]{2,4,3,1,0:T(8,128)}) %all-gather.2.cloned.1.call-update) | async-done | bytes 33554448 | tf_op jit(solution)/shard_map/all_gather | solution.py:56
  331.9 12.3 %reduce_sum.29 = f32[2,128,32,32]{1,3,2,0:T(8,128)S(1)} reduce(f32[32,2,128,32,32]{2,4,3,1,0:T(8,128)} %all-gather.2.cloned.1.call-done, f32[]{:T(128)} %constant.15.clone.1), dimensions={0}, to_apply=%region_2.3 | reduce | flops 8126464 | bytes 34603012 | tf_op jit(solution)/shard_map/reduce_sum | solution.py:56
  344.1 1.3 constant_dynamic-slice_fusion
  345.5 2.4 copy.45
  (3 shorter events, 0.1 us)
Async XLA Ops:
  7.2 1.6 copy-start
  10.3 7.4 %copy-start.2 = (s32[32]{0:T(128)S(1)}, s32[32]{0:T(128)}, u32[]{:S(2)}) copy-start(s32[32]{0:T(128)} %param.4) | copy-start | bytes 388
  10.3 8.9 %copy-start.3 = (s32[128]{0:T(128)S(1)}, s32[128]{0:T(128)}, u32[]{:S(2)}) copy-start(s32[128]{0:T(128)} %param.5) | copy-start | bytes 1540
  10.3 57.1 %all-to-all-start = ((f32[528,8,128]{2,0,1:T(8,128)}), f32[528,8,128]{2,0,1:T(8,128)}, u32[]{:S(2)}, u32[]{:S(2)}) async-start(f32[528,8,128]{2,0,1:T(8,128)} %copy_bitcast_fusion), calls=%async_computation | async-start | bytes 4325376 | tf_op jit(solution)/shard_map/all_to_all | solution.py:49
  17.7 314.2 %all-gather.2.cloned.1.call-start = ((), (), s32[]{:S(2)}) async-start(), calls=%async_computation.1 | async-start | bytes 34603008 | tf_op jit(solution)/shard_map/all_gather | solution.py:56
  103.1 11.4 %copy-start.1 = (f32[128,32,128]{2,0,1:T(8,128)}, f32[128,32,128]{2,0,1:T(8,128)S(1)}, u32[]{:S(2)}) copy-start(f32[128,32,128]{2,0,1:T(8,128)S(1)} %get-tuple-element.4) | copy-start | bytes 6291460
Sparse Core Ops, SparseCore 0:
  137.9 193.8 all-gather.1
